TPU v7x, 256 devices: a whole 4x4x8 slice. The times are simulated.
256 devices in a mesh: row: 16 (over z, core), col: 16 (over y, x).
Axes of the slice: x: 4, y: 4, z: 8, core: 2. Of those that a mesh axis runs over, the one named last changes fastest.
Arguments:
- inverse: float32 [5, 16, 5, 16, 256, 256], P(None, 'row', None, 'col')
- struct_first: int32 [32], replicated, may hold values from 0 to 79, as said below
- struct_second: int32 [16], replicated, may hold values from 0 to 79, as said below
- factor_first: float32 [32, 256, 256], P('row'), may hold values from -0.25 to 0.25
- factor_second: float32 [16, 256, 256], P('row'), may hold values from -0.25 to 0.25
- link_factor: float32 [256, 256], replicated, may hold values from -0.375 to 0.375
- dinv_first: float32 [256, 256], replicated, may hold values from -6 to 6
- dinv_second: float32 [256, 256], replicated, may hold values from -6 to 6
Outputs:
- column_first: float32 [5, 16, 256, 256], P(None, 'row', None, 'col')
- diag_first: float32 [256, 256], P(None, 'col')
- column_second: float32 [5, 16, 256, 256], P(None, 'row', None, 'col')
- link_second: float32 [256, 256], P(None, 'col')
- diag_second: float32 [256, 256], P(None, 'col')
Inputs may be any that keep to these rules, and one draw needn't show every extreme that they name: `struct_first`: distinct tile ids. `struct_second`: distinct tile ids, each of them also in struct_first.
All inputs are finite; a program needn't handle non-finite values.
Results may differ from a plain program's by a relative error of at most 0.0001.
Values sent between devices are 32-bit elements; how exact they have to be, the bound alone decides.
A program may use at most 128 MiB of HBM per device.

v0:
```python
import jax
import jax.numpy as jnp
from jax import lax
from jax.sharding import PartitionSpec as P

PRECISE = lax.Precision.HIGHEST


def body(
    inverse,
    struct_first,
    struct_second,
    factor_first,
    factor_second,
    link_factor,
    dinv_first,
    dinv_second,
):
    grid_rows = lax.axis_size("row")
    grid_cols = lax.axis_size("col")
    my_row = lax.axis_index("row")
    my_col = lax.axis_index("col")
    tile_rows, _, tile_cols, _, extent, _ = inverse.shape
    local_inv = inverse.reshape(tile_rows, tile_cols, extent, extent)
    col_width = extent // grid_cols
    offset = my_col * col_width
    col_tiles = jnp.arange(tile_cols, dtype=jnp.int32) * grid_cols + my_col
    row_tiles = jnp.arange(tile_rows, dtype=jnp.int32) * grid_rows + my_row

    def route(factor, tile_ids):
        block_in = lax.all_gather(factor, "row", axis=0, tiled=True)
        pick_col = (tile_ids[None, :] == col_tiles[:, None]).astype(jnp.float32)
        pick_row = (tile_ids[None, :] == row_tiles[:, None]).astype(jnp.float32)
        col_sel = jnp.einsum("bj,jxy->bxy", pick_col, block_in, precision=PRECISE)
        row_sel = jnp.einsum("aj,jxy->axy", pick_row, block_in, precision=PRECISE)
        return (col_sel, row_sel)

    def reduce_cols(stacked):
        summed = lax.psum(stacked, "col")
        return lax.dynamic_slice_in_dim(summed, offset, col_width, 2)

    col_first, row_first = route(factor_first, struct_first)
    product_first = jnp.einsum("abxy,byz->axz", local_inv, col_first, precision=PRECISE)
    panel_first = reduce_cols(product_first)
    owned_first = jnp.any(row_tiles[:, None] == struct_first[None, :], axis=1).astype(jnp.float32)
    column_first = -owned_first[:, None, None] * panel_first
    diag_terms = jnp.einsum("axy,axz->yz", row_first, panel_first, precision=PRECISE)
    diag_first = lax.dynamic_slice_in_dim(dinv_first, offset, col_width, 1) + lax.psum(
        diag_terms, "row"
    )
    col_second, row_second = route(factor_second, struct_second)
    link_rows = lax.dynamic_slice_in_dim(link_factor, offset, col_width, 0)
    product_second = jnp.einsum("abxy,byz->axz", local_inv, col_second, precision=PRECISE)
    product_second = product_second + jnp.einsum(
        "axw,wz->axz", column_first, link_rows, precision=PRECISE
    )
    link_term = jnp.dot(
        diag_first, link_rows, precision=PRECISE, preferred_element_type=jnp.float32
    )
    reduced = reduce_cols(jnp.concatenate([product_second, link_term[None]], axis=0))
    panel_second = reduced[:tile_rows]
    join_share = reduced[tile_rows]
    owned_second = jnp.any(row_tiles[:, None] == struct_second[None, :], axis=1).astype(jnp.float32)
    column_second = -owned_second[:, None, None] * panel_second
    turned_part = jnp.einsum("axw,axz->wz", column_first, row_second, precision=PRECISE)
    second_terms = jnp.einsum("axy,axz->yz", row_second, panel_second, precision=PRECISE)
    turned_sum, second_sum = lax.psum((turned_part, second_terms), "row")
    turned = lax.all_to_all(turned_sum, "col", split_axis=1, concat_axis=0, tiled=True)
    joined = turned + join_share
    link_second = -joined
    diag_second = lax.dynamic_slice_in_dim(dinv_second, offset, col_width, 1) + second_sum
    diag_second = diag_second + jnp.dot(
        link_factor.T, joined, precision=PRECISE, preferred_element_type=jnp.float32
    )
    out_shape = (tile_rows, 1, extent, col_width)
    return (
        column_first.reshape(out_shape),
        diag_first,
        column_second.reshape(out_shape),
        link_second,
        diag_second,
    )


def solution(mesh):
    placed = (
        P(None, "row", None, "col", None, None),
        P(),
        P(),
        P("row", None, None),
        P("row", None, None),
        P(),
        P(),
        P(),
    )
    return jax.shard_map(
        body,
        mesh=mesh,
        in_specs=placed,
        out_specs=(
            P(None, "row", None, "col"),
            P(None, "col"),
            P(None, "row", None, "col"),
            P(None, "col"),
            P(None, "col"),
        ),
        check_vma=False,
    )
```

profile of v0, /device:TPU:2, one launch (start us, length us, event | category | flops | bytes accessed | tf_op | source)
XLA Modules:
  0.0 435.4 jit_solution(15003734028828694786)
XLA Ops:
  7.2 0.0 copy-start
  7.2 0.0 all-gather.3.cloned.1.call-start
  7.2 0.7 all-gather.3.cloned.1.call-update
  7.9 0.0 all-gather.5.cloned.1.call-start
  8.0 0.7 all-gather.5.cloned.1.call-update
  8.7 0.0 all-reduce.4.cloned.1.call-start
  8.7 1.0 constant_dynamic-slice_fusion.1
  9.7 0.1 copy.56
  9.8 0.8 compare_reduce_fusion.1
  10.7 58.0 %all-gather.3.cloned.1.call-done = f32[32,256,256]{2,1,0:T(8,128)} async-done(((f32[2,256,256]{2,1,0:T(8,128)}), f32[32,256,256]{2,1,0:T(8,128)}) %all-gather.3.cloned.1.call-update) | async-done | bytes 8388624 | tf_op jit(solution)/shard_map/all_gather | solution.py:31
  68.7 10.6 %fusion.2 = f32[5,256,256]{2,0,1:T(8,128)S(1)} fusion(f32[32,256,256]{2,1,0:T(8,128)} %all-gather.3.cloned.1.call-done, s32[32]{0:T(128)} %param.9, s32[5]{0:T(128)S(1)} %fusion.62), kind=kOutput, calls=%fused_computation.2 | convolution fusion | flops 125829280 | bytes 9699476 | tf_op jit(solution)/shard_map/bj,jxy->bxy/dot_general | solution.py:34
  79.3 1.5 copy.35
  80.8 0.0 copy-start.4
  80.8 9.9 %fusion.12 = f32[5,256,256]{1,2,0:T(8,128)} fusion(f32[5,1,5,1,256,256]{5,4,3,2,1,0:T(8,128)} %param.8, f32[5,256,256]{1,2,0:T(8,128)} %copy.35), kind=kOutput, calls=%fused_computation.13 | convolution fusion | flops 5033164800 | bytes 9175040 | tf_op jit(solution)/shard_map/abxy,byz->axz/dot_general | solution.py:43
  90.8 0.0 all-reduce.4.cloned.1.call-update
  90.8 10.8 %all-reduce.6.cloned.1.call-start = ((), (), s32[]{:S(2)}) async-start(), calls=%async_computation.4 | async-start | bytes 3145728 | tf_op jit(solution)/shard_map/psum | solution.py:39
  101.6 9.4 %all-gather.5.cloned.1.call-done = f32[16,256,256]{2,1,0:T(8,128)} async-done(((f32[1,256,256]{2,1,0:T(8,128)}), f32[16,256,256]{2,1,0:T(8,128)}) %all-gather.5.cloned.1.call-update) | async-done | bytes 4194320 | tf_op jit(solution)/shard_map/all_gather | solution.py:31
  111.0 0.0 copy-done.4
  111.0 5.8 %fusion.10 = f32[5,256,256]{2,0,1:T(8,128)S(1)} fusion(f32[16,256,256]{2,1,0:T(8,128)} %all-gather.5.cloned.1.call-done, s32[16]{0:T(128)S(1)} %copy-done.4, s32[5]{0:T(128)S(1)} %fusion.62), kind=kOutput, calls=%fused_computation.10 | convolution fusion | flops 62914640 | bytes 5505108 | tf_op jit(solution)/shard_map/bj,jxy->bxy/dot_general | solution.py:34
  116.8 1.5 copy.40
  118.3 0.0 copy-start.3
  118.3 10.0 %fusion.15 = f32[5,256,256]{1,2,0:T(8,128)} fusion(f32[5,1,5,1,256,256]{5,4,3,2,1,0:T(8,128)} %param.8, f32[5,256,256]{1,2,0:T(8,128)} %copy.40), kind=kOutput, calls=%fused_computation.14 | convolution fusion | flops 5033164800 | bytes 9175040 | tf_op jit(solution)/shard_map/abxy,byz->axz/dot_general | solution.py:53
  128.3 0.0 copy-done.3
  128.3 10.7 %fusion = f32[5,256,256]{2,0,1:T(8,128)S(1)} fusion(f32[32,256,256]{2,1,0:T(8,128)} %all-gather.3.cloned.1.call-done, s32[32]{0:T(128)S(1)} %copy-done.3, s32[5]{0:T(128)S(1)} %fusion.63), kind=kOutput, calls=%fused_computation | convolution fusion | flops 125829280 | bytes 9699476 | tf_op jit(solution)/shard_map/aj,jxy->axy/dot_general | solution.py:35
  139.0 71.3 %all-reduce.4.cloned.1.call-done = f32[5,256,256]{1,2,0:T(8,128)} async-done(((f32[5,256,256]{1,2,0:T(8,128)}), f32[5,256,256]{1,2,0:T(8,128)}) %all-reduce.4.cloned.1.call-update) | async-done | bytes 1310736 | tf_op jit(solution)/shard_map/psum | solution.py:39
  210.4 1.9 fusion.22
  212.3 46.3 %psum.36 = f32[256,16]{0,1:T(8,128)S(1)} all-reduce(f32[256,16]{0,1:T(8,128)S(1)} %fusion.22), channel_id=1, replica_groups=mesh['row'=16,'col'=16] {'row'}, use_global_device_ids=true, to_apply=%region_2.0 | all-reduce | flops 4096 | bytes 32768 | tf_op jit(solution)/shard_map/psum | solution.py:48
  258.5 0.0 copy-done
  258.5 0.0 copy-start.1
  258.5 0.4 convolution_bitcast_fusion
  259.0 2.6 convolution_add_fusion
  261.6 1.2 pad_maximum_fusion
  262.8 0.0 copy-done.1
  262.9 0.0 copy-start.2
  262.9 0.0 all-reduce.6.cloned.1.call-update
  262.9 0.9 copy-done.2
  263.8 0.1 constant_dynamic-slice_fusion
  263.9 0.1 copy.57
  264.0 0.2 compare_reduce_fusion
  264.2 5.8 %fusion.8 = f32[5,256,256]{2,0,1:T(8,128)S(1)} fusion(f32[16,256,256]{2,1,0:T(8,128)} %all-gather.5.cloned.1.call-done, s32[16]{0:T(128)S(1)} %copy-done.4, s32[5]{0:T(128)S(1)} %fusion.63), kind=kOutput, calls=%fused_computation.8 | convolution fusion | flops 62914640 | bytes 5505108 | tf_op jit(solution)/shard_map/aj,jxy->axy/dot_general | solution.py:35
  270.0 1.6 fusion.31
  271.6 3.2 fusion.27
  274.9 86.3 %all-reduce.6.cloned.1.call-done = f32[6,256,256]{1,2,0:T(8,128)} async-done(((f32[6,256,256]{1,2,0:T(8,128)}), f32[6,256,256]{1,2,0:T(8,128)}) %all-reduce.6.cloned.1.call-update) | async-done | bytes 1572880 | tf_op jit(solution)/shard_map/psum | solution.py:39
  361.2 1.9 convolution_bitcast_fusion.1
  363.1 48.2 %all-reduce = (f32[16,16,16]{0,2,1:T(8,128)S(1)}, f32[256,16]{0,1:T(8,128)S(1)}) all-reduce(f32[16,16,16]{0,2,1:T(8,128)S(1)} %bitcast.78, f32[256,16]{0,1:T(8,128)S(1)} %convolution_bitcast_fusion.1), channel_id=1, replica_groups=mesh['row'=16,'col'=16] {'row'}, use_global_device_ids=true, to_apply=%region_5.0 | all-reduce | flops 8192 | bytes 65536 | tf_op jit(solution)/shard_map/psum | solution.py:67
  411.3 0.7 reshape.57
  412.0 5.9 %all-to-all-start = ((f32[16,1,256]{2,1,0:T(1,128)}), f32[16,1,256]{2,1,0:T(1,128)S(1)}, u32[]{:S(2)}, u32[]{:S(2)}) async-start(f32[16,1,256]{2,1,0:T(1,128)} %reshape.57), calls=%async_computation | async-start | bytes 32768 | tf_op jit(solution)/shard_map/all_to_all | solution.py:68
  417.9 1.6 multiply_bitcast_fusion
  419.5 4.6 %all-to-all-done = f32[16,1,256]{2,1,0:T(1,128)S(1)} async-done(((f32[16,1,256]{2,1,0:T(1,128)}), f32[16,1,256]{2,1,0:T(1,128)S(1)}, u32[]{:S(2)}, u32[]{:S(2)}) %all-to-all-start) | async-done | bytes 16416 | tf_op jit(solution)/shard_map/all_to_all | solution.py:68
  424.1 0.5 broadcast.23
  424.6 0.7 reduce
  425.3 0.1 reshape.58
  425.5 0.1 all_to_all.17
  425.6 1.3 fusion.39
  426.9 1.6 fusion.25
  (7 shorter events, 0.1 us)
Async XLA Ops:
  7.2 251.4 %copy-start = (f32[256,256]{1,0:T(8,128)S(1)}, f32[256,256]{1,0:T(8,128)}, u32[]{:S(2)}) copy-start(f32[256,256]{1,0:T(8,128)} %param.13) | copy-start | bytes 786436
  7.2 61.5 %all-gather.3.cloned.1.call-start = ((), (), s32[]{:S(2)}) async-start(), calls=%async_computation.1 | async-start | bytes 8912896 | tf_op jit(solution)/shard_map/all_gather | solution.py:31
  7.9 103.0 %all-gather.5.cloned.1.call-start = ((), (), s32[]{:S(2)}) async-start(), calls=%async_computation.3 | async-start | bytes 4456448 | tf_op jit(solution)/shard_map/all_gather | solution.py:31
  8.7 201.7 %all-reduce.4.cloned.1.call-start = ((), (), s32[]{:S(2)}) async-start(), calls=%async_computation.2 | async-start | bytes 2621440 | tf_op jit(solution)/shard_map/psum | solution.py:39
  80.8 30.1 %copy-start.4 = (s32[16]{0:T(128)S(1)}, s32[16]{0:T(128)}, u32[]{:S(2)}) copy-start(s32[16]{0:T(128)} %param.10) | copy-start | bytes 196
  90.8 270.4 %all-reduce.6.cloned.1.call-start = ((), (), s32[]{:S(2)}) async-start(), calls=%async_computation.4 | async-start | bytes 3145728 | tf_op jit(solution)/shard_map/psum | solution.py:39
  118.3 10.0 %copy-start.3 = (s32[32]{0:T(128)S(1)}, s32[32]{0:T(128)}, u32[]{:S(2)}) copy-start(s32[32]{0:T(128)} %param.9) | copy-start | bytes 388
  258.5 4.3 copy-start.1
  262.9 1.0 copy-start.2
  412.0 12.1 %all-to-all-start = ((f32[16,1,256]{2,1,0:T(1,128)}), f32[16,1,256]{2,1,0:T(1,128)S(1)}, u32[]{:S(2)}, u32[]{:S(2)}) async-start(f32[16,1,256]{2,1,0:T(1,128)} %reshape.57), calls=%async_computation | async-start | bytes 32768 | tf_op jit(solution)/shard_map/all_to_all | solution.py:68
Sparse Core Ops, SparseCore 0:
  9.8 58.7 all-gather.2
  70.5 40.4 all-gather.4
  114.2 96.1 all-reduce.3
  263.0 98.1 all-reduce.5
where the time goes:
time: 444 us; the launch traced here: 435 us
  waiting for transfers between devices  231 us (52%)
  blocking collectives  94.4 us (21%)
  matrix products  64.5 us (15%)
  starting transfers between devices  16.8 us (4%)
  between operations  14.3 us (3%)
  other arithmetic  7.53 us (2%)
  local copies, waits for them, and re-layouts  6.73 us (2%)
    psum x2, waiting for transfers between devices, reduce_cols(): summed = lax.psum(stacked, 'col')  158 us
    all_gather x2, waiting for transfers between devices, route(): block_in = lax.all_gather(factor, 'row', axis=0, tiled=True)  67.4 us
    psum x1, blocking collectives, body(): turned_sum, second_sum = lax.psum((turned_part, second_terms), 'row')  48.2 us
    psum x1, blocking collectives, body(): lax.psum(diag_terms, 'row')  46.3 us
    dot_general x2, matrix products, route(): row_sel = jnp.einsum('aj,jxy->axy', pick_row, block_in, precision=PRECISE)  16.6 us
    dot_general x2, matrix products, route(): col_sel = jnp.einsum('bj,jxy->bxy', pick_col, block_in, precision=PRECISE)  16.5 us
    psum x2, starting transfers between devices, reduce_cols(): summed = lax.psum(stacked, 'col')  10.8 us
    dot_general x1, matrix products, body(): jnp.einsum('abxy,byz->axz', local_inv, col_second, precision=PRECISE)  9.96 us
  transfers between devices with their start and end apart: 5, of which 5 were waited for; matrix products, arithmetic and copies ran while one was open for 15% of the time, Pallas kernels for 0%

commit v1 on v0

--- a/solution.py
+++ b/solution.py
@@ -4,6 +4,12 @@
 from jax.sharding import PartitionSpec as P
 
 PRECISE = lax.Precision.HIGHEST
+_see_teams = lambda frame, named_axis: jnp.concatenate(
+    lax.all_to_all(
+        jnp.stack([frame] * lax.axis_size(named_axis)), named_axis, split_axis=0, concat_axis=0
+    ),
+    axis=0,
+)
 
 
 def body(
@@ -28,7 +34,7 @@
     row_tiles = jnp.arange(tile_rows, dtype=jnp.int32) * grid_rows + my_row
 
     def route(factor, tile_ids):
-        block_in = lax.all_gather(factor, "row", axis=0, tiled=True)
+        block_in = _see_teams(factor, "row")
         pick_col = (tile_ids[None, :] == col_tiles[:, None]).astype(jnp.float32)
         pick_row = (tile_ids[None, :] == row_tiles[:, None]).astype(jnp.float32)
         col_sel = jnp.einsum("bj,jxy->bxy", pick_col, block_in, precision=PRECISE)

time: 444 us -> 578 us (1.30); the launches traced: 435 us -> 576 us
  blocking collectives: 94.4 us -> 288 us
  waiting for transfers between devices: 231 us -> 167 us
  local copies, waits for them, and re-layouts: 6.73 us -> 35.6 us
  matrix products: 64.5 us -> 53.5 us
    all_to_all x0 -> x1, blocking collectives: none -> 193 us  [lax.all_to_all(jnp.stack([frame] * lax.axis_size(named_axis)), named_axis...]
    all_gather x2 -> x0, waiting for transfers between devices: 67.4 us -> none  [route(): block_in = lax.all_gather(factor, 'row', axis=0, tiled=True)]
    all_to_all x0 -> x1, waiting for transfers between devices: none -> 57.1 us  [lax.all_to_all(jnp.stack([frame] * lax.axis_size(named_axis)), named_axis...]
    psum x2, waiting for transfers between devices: 158 us -> 106 us  [reduce_cols(): summed = lax.psum(stacked, 'col')]
    reshape x0 -> x1, local copies, waits for them, and re-layouts: none -> 10.9 us  [jnp.concatenate(lax.all_to_all(jnp.stack([frame] * lax.axis_size(named_ax...]
    psum x2, starting transfers between devices: 10.8 us -> 0.48 us  [reduce_cols(): summed = lax.psum(stacked, 'col')]
    another operation x0 -> x2, local copies, waits for them, and re-layouts: none -> 8.82 us  [jnp.stack([frame] * lax.axis_size(named_axis))]
    all_to_all x0 -> x1, local copies, waits for them, and re-layouts: none -> 8.58 us  [lax.all_to_all(jnp.stack([frame] * lax.axis_size(named_axis)), named_axis...]
  transfers between devices with their start and end apart: 5 -> 4, of which waited for: 5 -> 4; matrix products, arithmetic and copies ran while one was open for 15% -> 12% of each run, Pallas kernels for 0% -> 0%
where the time goes in v1:
time: 578 us; the launch traced here: 576 us
  blocking collectives  288 us (50%)
  waiting for transfers between devices  167 us (29%)
  matrix products  53.5 us (9%)
  local copies, waits for them, and re-layouts  35.6 us (6%)
  between operations  14.2 us (2%)
  starting transfers between devices  11.1 us (2%)
  other arithmetic  6.87 us (1%)
    all_to_all x1, blocking collectives, lax.all_to_all(jnp.stack([frame] * lax.axis_size(named_axis)), named_axis...  193 us
    psum x2, waiting for transfers between devices, reduce_cols(): summed = lax.psum(stacked, 'col')  106 us
    all_to_all x1, waiting for transfers between devices, lax.all_to_all(jnp.stack([frame] * lax.axis_size(named_axis)), named_axis...  57.1 us
    psum x1, blocking collectives, body(): turned_sum, second_sum = lax.psum((turned_part, second_terms), 'row')  48.2 us
    psum x1, blocking collectives, body(): lax.psum(diag_terms, 'row')  46.3 us
  transfers between devices with their start and end apart: 4, of which 4 were waited for; matrix products, arithmetic and copies ran while one was open for 12% of the time, Pallas kernels for 0%

profile of v1, /device:TPU:2, one launch (start us, length us, event | category | flops | bytes accessed | tf_op | source)
XLA Modules:
  0.0 576.4 jit_solution(18099234665986417335)
XLA Ops:
  7.2 0.0 copy-start
  7.2 1.5 copy.48
  8.7 6.4 %stack.4 = f32[16,2,256,256]{3,1,2,0:T(2,128)} broadcast(f32[2,256,256]{2,0,1:T(2,128)S(1)} %copy.48), dimensions={1,2,3} | broadcast | bytes 8912896 | tf_op jit(solution)/shard_map/stack | solution.py:9
  15.1 0.0 copy-start.1
  15.1 193.3 %all_to_all.29 = f32[16,2,256,256]{3,1,2,0:T(2,128)} all-to-all(f32[16,2,256,256]{3,1,2,0:T(2,128)} %stack.4), channel_id=1, replica_groups=mesh['row'=16,'col'=16] {'row'}, dimensions={0} | all-to-all | bytes 16777216 | tf_op jit(solution)/shard_map/all_to_all | solution.py:8
  208.4 0.0 copy-done.1
  208.4 2.4 stack.5
  210.8 0.0 copy-start.3
  210.8 0.0 copy-start.5
  210.8 4.7 all-to-all-start.1
  215.5 0.2 all-reduce.4.cloned.1.call-start
  215.7 0.0 copy-done.3
  215.7 0.1 constant_dynamic-slice_fusion.1
  215.8 0.1 copy.69
  215.9 0.0 copy-done.5
  215.9 0.2 compare_reduce_fusion.1
  216.1 8.6 %copy.49 = f32[16,2,256,256]{3,1,0,2:T(2,128)} copy(f32[16,2,256,256]{3,1,2,0:T(2,128)} %all_to_all.29) | data formatting | bytes 16777216 | tf_op jit(solution)/shard_map/all_to_all | solution.py:8
  224.7 10.9 %reshape.53 = f32[32,256,256]{2,0,1:T(8,128)} reshape(f32[16,2,256,256]{3,1,0,2:T(2,128)} %copy.49) | data formatting | bytes 16777216 | tf_op jit(solution)/shard_map/reshape | solution.py:7
  235.5 5.2 fusion.42
  240.7 1.6 copy.50
  242.3 0.0 copy-start.6
  242.3 10.0 %fusion.10 = f32[5,256,256]{1,2,0:T(8,128)} fusion(f32[5,1,5,1,256,256]{5,4,3,2,1,0:T(8,128)} %param.8, f32[5,256,256]{1,2,0:T(8,128)} %copy.50), kind=kOutput, calls=%fused_computation.11 | convolution fusion | flops 5033164800 | bytes 9175040 | tf_op jit(solution)/shard_map/abxy,byz->axz/dot_general | solution.py:49
  252.2 0.0 all-reduce.4.cloned.1.call-update
  252.3 0.3 all-reduce.6.cloned.1.call-start
  252.5 57.1 %all-to-all-done.1 = f32[16,1,256,256]{3,2,1,0:T(8,128)} async-done(((f32[16,1,256,256]{3,2,1,0:T(8,128)}), f32[16,1,256,256]{3,2,1,0:T(8,128)}, u32[]{:S(2)}, u32[]{:S(2)}) %all-to-all-start.1) | async-done | bytes 4194336 | tf_op jit(solution)/shard_map/all_to_all | solution.py:8
  309.7 0.0 copy-done.6
  309.7 5.9 %fusion.6 = f32[5,256,256]{2,0,1:T(8,128)S(1)} fusion(f32[16,1,256,256]{3,2,1,0:T(8,128)} %all-to-all-done.1, s32[16]{0:T(128)S(1)} %copy-done.6, s32[5]{0:T(128)S(1)} %fusion.62), kind=kOutput, calls=%fused_computation.6 | convolution fusion | flops 62914640 | bytes 5505108 | tf_op jit(solution)/shard_map/bj,jxy->bxy/dot_general | solution.py:40
  315.5 1.5 copy.54
  317.1 9.9 %fusion.13 = f32[5,256,256]{1,2,0:T(8,128)} fusion(f32[5,1,5,1,256,256]{5,4,3,2,1,0:T(8,128)} %param.8, f32[5,256,256]{1,2,0:T(8,128)} %copy.54), kind=kOutput, calls=%fused_computation.12 | convolution fusion | flops 5033164800 | bytes 9175040 | tf_op jit(solution)/shard_map/abxy,byz->axz/dot_general | solution.py:59
  327.0 5.2 fusion.40
  332.2 19.3 %all-reduce.4.cloned.1.call-done = f32[5,256,256]{1,2,0:T(8,128)} async-done(((f32[5,256,256]{1,2,0:T(8,128)}), f32[5,256,256]{1,2,0:T(8,128)}) %all-reduce.4.cloned.1.call-update) | async-done | bytes 1310736 | tf_op jit(solution)/shard_map/psum | solution.py:45
  351.4 1.9 fusion.20
  353.3 46.3 %psum.36 = f32[256,16]{0,1:T(8,128)S(1)} all-reduce(f32[256,16]{0,1:T(8,128)S(1)} %fusion.20), channel_id=1, replica_groups=mesh['row'=16,'col'=16] {'row'}, use_global_device_ids=true, to_apply=%region_2.0 | all-reduce | flops 4096 | bytes 32768 | tf_op jit(solution)/shard_map/psum | solution.py:54
  399.6 0.0 copy-done
  399.6 0.0 copy-start.2
  399.6 0.4 convolution_bitcast_fusion
  400.0 2.6 convolution_add_fusion
  402.6 1.2 pad_maximum_fusion
  403.9 0.0 copy-done.2
  403.9 0.0 copy-start.4
  403.9 0.0 all-reduce.6.cloned.1.call-update
  403.9 0.9 copy-done.4
  404.9 0.1 constant_dynamic-slice_fusion
  405.0 0.1 copy.70
  405.0 0.2 compare_reduce_fusion
  405.2 5.8 %fusion.4 = f32[5,256,256]{2,0,1:T(8,128)S(1)} fusion(f32[16,1,256,256]{3,2,1,0:T(8,128)} %all-to-all-done.1, s32[16]{0:T(128)S(1)} %copy-done.6, s32[5]{0:T(128)S(1)} %fusion.63), kind=kOutput, calls=%fused_computation.4 | convolution fusion | flops 62914640 | bytes 5505108 | tf_op jit(solution)/shard_map/aj,jxy->axy/dot_general | solution.py:41
  411.1 1.6 fusion.29
  412.7 3.2 fusion.25
  415.9 86.4 %all-reduce.6.cloned.1.call-done = f32[6,256,256]{1,2,0:T(8,128)} async-done(((f32[6,256,256]{1,2,0:T(8,128)}), f32[6,256,256]{1,2,0:T(8,128)}) %all-reduce.6.cloned.1.call-update) | async-done | bytes 1572880 | tf_op jit(solution)/shard_map/psum | solution.py:45
  502.3 1.9 convolution_bitcast_fusion.1
  504.2 48.2 %all-reduce = (f32[16,16,16]{0,2,1:T(8,128)S(1)}, f32[256,16]{0,1:T(8,128)S(1)}) all-reduce(f32[16,16,16]{0,2,1:T(8,128)S(1)} %bitcast.88, f32[256,16]{0,1:T(8,128)S(1)} %convolution_bitcast_fusion.1), channel_id=1, replica_groups=mesh['row'=16,'col'=16] {'row'}, use_global_device_ids=true, to_apply=%region_5.0 | all-reduce | flops 8192 | bytes 65536 | tf_op jit(solution)/shard_map/psum | solution.py:73
  552.4 0.7 reshape.70
  553.1 5.9 %all-to-all-start.2 = ((f32[16,1,256]{2,1,0:T(1,128)}), f32[16,1,256]{2,1,0:T(1,128)S(1)}, u32[]{:S(2)}, u32[]{:S(2)}) async-start(f32[16,1,256]{2,1,0:T(1,128)} %reshape.70), calls=%async_computation.2 | async-start | bytes 32768 | tf_op jit(solution)/shard_map/all_to_all | solution.py:74
  559.0 1.6 multiply_bitcast_fusion
  560.6 4.6 all-to-all-done.2
  565.2 0.5 broadcast.28
  565.7 0.7 reduce
  566.4 0.1 reshape.71
  566.6 0.1 all_to_all.25
  566.7 1.3 fusion.37
  568.0 1.6 fusion.23
  (7 shorter events, 0.1 us)
Async XLA Ops:
  7.2 392.4 %copy-start = (f32[256,256]{1,0:T(8,128)S(1)}, f32[256,256]{1,0:T(8,128)}, u32[]{:S(2)}) copy-start(f32[256,256]{1,0:T(8,128)} %param.13) | copy-start | bytes 786436
  15.1 193.3 %copy-start.1 = (f32[1,256,256]{2,1,0:T(8,128)S(1)}, f32[1,256,256]{2,1,0:T(8,128)}, u32[]{:S(2)}) copy-start(f32[1,256,256]{2,1,0:T(8,128)} %param.12) | copy-start | bytes 786436
  210.8 4.9 copy-start.3
  210.8 5.1 copy-start.5
  210.8 98.9 %all-to-all-start.1 = ((f32[16,1,256,256]{3,2,1,0:T(8,128)}), f32[16,1,256,256]{3,2,1,0:T(8,128)}, u32[]{:S(2)}, u32[]{:S(2)}) async-start(f32[16,1,256,256]{3,2,1,0:T(8,128)} %stack.5), calls=%async_computation.1 | async-start | bytes 8388608 | tf_op jit(solution)/shard_map/all_to_all | solution.py:8
  215.5 136.0 %all-reduce.4.cloned.1.call-start = ((), (), s32[]{:S(2)}) async-start(), calls=%async_computation.3 | async-start | bytes 2621440 | tf_op jit(solution)/shard_map/psum | solution.py:45
  242.3 67.4 %copy-start.6 = (s32[16]{0:T(128)S(1)}, s32[16]{0:T(128)}, u32[]{:S(2)}) copy-start(s32[16]{0:T(128)} %param.10) | copy-start | bytes 196
  252.3 250.0 %all-reduce.6.cloned.1.call-start = ((), (), s32[]{:S(2)}) async-start(), calls=%async_computation.4 | async-start | bytes 3145728 | tf_op jit(solution)/shard_map/psum | solution.py:45
  399.6 4.3 copy-start.2
  403.9 1.0 copy-start.4
  553.1 12.1 %all-to-all-start.2 = ((f32[16,1,256]{2,1,0:T(1,128)}), f32[16,1,256]{2,1,0:T(1,128)S(1)}, u32[]{:S(2)}, u32[]{:S(2)}) async-start(f32[16,1,256]{2,1,0:T(1,128)} %reshape.70), calls=%async_computation.2 | async-start | bytes 32768 | tf_op jit(solution)/shard_map/all_to_all | solution.py:74
Sparse Core Ops, SparseCore 0:
  252.4 98.9 all-reduce.3
  404.0 98.1 all-reduce.5
